TPU v7x, 32 devices: a whole 2x2x4 slice. The times are simulated.
32 devices in a mesh: mem: 4 (over y, x), sp: 8 (over z, core).
Axes of the slice: x: 2, y: 2, z: 4, core: 2. Of those that a mesh axis runs over, the one named last changes fastest.
Arguments:
- member_predictors: bfloat16 [32, 8, 16, 128], P('mem', None, 'sp'), may hold values from -6 to 6
- member_skill_logit: bfloat16 [32, 16, 128], P('mem', 'sp'), may hold values from -8 to 250
- opening_filter: bfloat16 [9, 8, 128], replicated, may hold values from -0.75 to 0.75
- opening_bias: float32 [128], replicated, may hold values from -3 to 3
- following_filter: bfloat16 [9, 128, 128], replicated, may hold values from -0.1875 to 0.1875
- layer_norm_scales: float32 [2, 2, 128], replicated, may hold values from 0.5 to 1.5
- query_key_value_weight: bfloat16 [2, 128, 384], replicated, may hold values from -0.5 to 0.5
- attention_output_weight: bfloat16 [2, 128, 128], replicated, may hold values from -0.5 to 0.5
- upward_weight: bfloat16 [2, 128, 512], replicated, may hold values from -0.5 to 0.5
- downward_weight: bfloat16 [2, 512, 128], replicated, may hold values from -0.25 to 0.25
- closing_norm_scale: float32 [128], replicated, may hold values from 0.5 to 1.5
- readout_weight: bfloat16 [128, 2], replicated, may hold values from -0.5 to 0.5
Outputs:
- corrected: float32 [32, 2, 16, 128], P('mem', None, 'sp')
All inputs are finite; a program needn't handle non-finite values.
Results may differ from a plain program's by a relative error of at most 0.012.
Values may be sent and summed in bfloat16 or wider, within the bound.
A program may use at most 64 MiB of HBM per device.

v0:
```python
import functools
import math

import jax
import jax.numpy as jnp
from jax import lax
from jax.experimental import pallas as pl
from jax.experimental.pallas import tpu as pltpu
from jax.sharding import PartitionSpec as P

CORRECTED_COUNT = 2
HEADS = 8
LAYERS = 2
LANES = 128
BLOCK = 256


def extended(cells, axis, dim, width):
    count = lax.axis_size(axis)
    ends = count - 1
    head = lax.slice_in_dim(cells, 0, width, axis=dim)
    tail = lax.slice_in_dim(cells, cells.shape[dim] - width, cells.shape[dim], axis=dim)
    return jnp.concatenate(
        [
            lax.ppermute(tail, axis, [(i, (i + 1) % count) for i in range(ends)]),
            cells,
            lax.ppermute(head, axis, [((i + 1) % count, i) for i in range(ends)]),
        ],
        axis=dim,
    )


def norm_columns(stream, gain):
    average = jnp.mean(stream, 0, keepdims=True)
    centred = stream - average
    variance = jnp.mean(centred * centred, 0, keepdims=True)
    return (centred * lax.rsqrt(variance + 1e-05) * gain).astype(jnp.bfloat16)


def dot(left, right):
    return jnp.dot(left, right, preferred_element_type=jnp.float32)


def dot_first(left, right):
    return lax.dot_general(left, right, (((0,), (0,)), ((), ())), preferred_element_type=jnp.float32)


def flipped(weight):
    return weight.astype(jnp.float32).T.astype(jnp.bfloat16)


def kernel(
    sizes,
    place,
    patches,
    bias,
    opening,
    opening_bias,
    following,
    gains,
    qkv,
    out_weight,
    up,
    down,
    readout,
    result,
    first,
    qkv_t,
    out_t,
    up_t,
    down_t,
    triple,
    attended,
):
    members, row_count, col_count, col_span, row_total, col_total = sizes
    width = opening.shape[2]
    head = width // HEADS
    lanes = patches.shape[2]
    step = pl.program_id(0)

    @pl.when(step == 0)
    def _():
        for layer in range(LAYERS):
            qkv_t[layer] = flipped(qkv[layer])
            out_t[layer] = flipped(out_weight[layer])
            up_t[layer] = flipped(up[layer])
            down_t[layer] = flipped(down[layer])
        chunk = next(c for c in (384, 256, 128) if lanes % c == 0)
        for row in range(row_count + 2):
            row_id = place[0] - 1 + row
            row_fits = (row_id >= 0) & (row_id < row_total)

            def widen(i, carry):
                start = pl.multiple_of(i * chunk, chunk)
                total = jnp.zeros((chunk, width), jnp.float32) + opening_bias[...]
                for off in range(3):
                    total = total + dot_first(patches[row + off, :, pl.ds(start, chunk)], opening[off])
                col_id = place[1] - 1 + (start + lax.broadcasted_iota(jnp.int32, total.shape, 0)) // members
                fits = (col_id >= 0) & (col_id < col_total) & row_fits
                value = jnp.where(fits, jax.nn.gelu(total), 0.0)
                first[pl.ds(pl.multiple_of(row * lanes + start, 128), chunk), :] = value.astype(jnp.bfloat16)
                return carry

            lax.fori_loop(0, lanes // chunk, widen, 0)

    cells = BLOCK // members
    row = (step * cells) // col_count
    col = (step * cells) % col_count

    def shifted(row_off, col_off):
        start = ((row + row_off) * col_span + col + col_off) * members
        return first[pl.ds(pl.multiple_of(start, members), BLOCK), :]

    features = shifted(1, 1).astype(jnp.float32)
    summed = jnp.zeros((BLOCK, width), jnp.float32)
    for tap in range(9):
        summed = summed + dot(shifted(tap // 3, tap % 3), following[tap])
    stream = (features + summed).astype(jnp.bfloat16).astype(jnp.float32).T

    each = LANES // members
    owner = lax.broadcasted_iota(jnp.int32, (members, LANES), 1) // members
    holds = [owner == c for c in range(each)]
    keeps = [jnp.where(hold, 1.0, 0.0).astype(jnp.bfloat16) for hold in holds]
    scale = 1.0 / math.sqrt(head)
    for layer in range(LAYERS):
        normed = norm_columns(stream, gains[:, 2 * layer : 2 * layer + 1])
        triple[...] = dot(qkv_t[layer], normed).astype(jnp.bfloat16)
        for group in range(BLOCK // LANES):
            at = slice(group * LANES, (group + 1) * LANES)
            offset = bias[group].astype(jnp.float32)
            for h in range(HEADS):
                rows = slice(h * head, (h + 1) * head)
                queries = triple[h * head : (h + 1) * head, at]
                keys = triple[width + h * head : width + (h + 1) * head, at]
                values = triple[2 * width + h * head : 2 * width + (h + 1) * head, at]
                every = dot_first(keys, queries)
                scores = every[:members]
                for c in range(1, each):
                    scores = jnp.where(holds[c], every[c * members : (c + 1) * members], scores)
                scores = scores * scale + offset
                raised = jnp.exp(scores - jnp.max(scores, 0, keepdims=True))
                weights = (raised * (1.0 / jnp.sum(raised, 0, keepdims=True))).astype(jnp.bfloat16)
                spread = jnp.concatenate([weights * keep for keep in keeps], axis=0)
                attended[rows, at] = dot(values, spread).astype(jnp.bfloat16)
        stream = stream + dot(out_t[layer], attended[...])
        normed = norm_columns(stream, gains[:, 2 * layer + 1 : 2 * layer + 2])
        hidden = jax.nn.gelu(dot(up_t[layer], normed)).astype(jnp.bfloat16)
        stream = stream + dot(down_t[layer], hidden)
    final = norm_columns(stream, gains[:, 2 * LAYERS : 2 * LAYERS + 1])
    result[...] = dot(readout[...], final)[: result.shape[0]]


def shards(
    member_predictors,
    member_skill_logit,
    opening_filter,
    opening_bias,
    following_filter,
    layer_norm_scales,
    query_key_value_weight,
    attention_output_weight,
    upward_weight,
    downward_weight,
    closing_norm_scale,
    readout_weight,
):
    held, fields, row_span, col_total = member_predictors.shape
    groups = lax.axis_size("mem")
    members = held * groups
    cols = col_total // groups
    row_total = row_span * lax.axis_size("sp")
    width = opening_filter.shape[2]
    place = jnp.stack([lax.axis_index("sp") * row_span, lax.axis_index("mem") * cols]).astype(jnp.int32)

    padded = extended(member_predictors, "sp", 2, 2)
    padded = jnp.pad(padded, ((0, 0), (0, 0), (0, 0), (2, 2)))
    parcels = jnp.stack(
        [
            jnp.concatenate(
                [
                    padded[:, :, :, k * cols : (k + 1) * cols + 4].reshape(held, -1),
                    member_skill_logit[:, :, k * cols : (k + 1) * cols].reshape(held, -1),
                ],
                axis=1,
            )
            for k in range(groups)
        ]
    )
    parcels = lax.all_to_all(parcels, "mem", split_axis=0, concat_axis=0, tiled=True)
    parcels = parcels.reshape(members, -1)
    rows = row_span + 4
    cut = fields * rows * (cols + 4)
    local = parcels[:, :cut].reshape(members, fields, rows, cols + 4)
    logits = parcels[:, cut:].reshape(members, row_span * cols)

    lanes = -(-(cols + 2) * members // LANES) * LANES
    col_span = lanes // members
    local = local.transpose(2, 1, 3, 0).reshape(rows, fields, (cols + 4) * members)
    local = jnp.pad(local, ((0, 0), (0, 0), (0, max(0, lanes - (cols + 2) * members))))
    patches = jnp.concatenate(
        [local[:, :, off * members : off * members + lanes] for off in range(3)], axis=1
    )
    opening = opening_filter.reshape(3, 3 * fields, width)
    each = LANES // members
    bias = logits.reshape(members, -1, each).transpose(1, 0, 2)
    bias = jnp.repeat(bias, members, axis=2)
    gains = jnp.concatenate(
        [layer_norm_scales.reshape(2 * LAYERS, width), closing_norm_scale[None]], axis=0
    )
    gains = jnp.pad(gains, ((0, 8 - gains.shape[0]), (0, 0))).T
    readout = jnp.pad(readout_weight.T, ((0, 16 - readout_weight.shape[1]), (0, 0)))

    tokens = row_span * cols * members
    sizes = (members, row_span, cols, col_span, row_total, col_total)
    whole = pl.BlockSpec(memory_space=pltpu.VMEM)
    ff = upward_weight.shape[2]
    correction = pl.pallas_call(
        functools.partial(kernel, sizes),
        grid=(tokens // BLOCK,),
        out_shape=jax.ShapeDtypeStruct((CORRECTED_COUNT, tokens), jnp.float32),
        in_specs=[
            pl.BlockSpec(memory_space=pltpu.SMEM),
            whole,
            pl.BlockSpec((BLOCK // LANES, members, LANES), lambda i: (i, 0, 0)),
        ]
        + [whole] * 9,
        out_specs=pl.BlockSpec((CORRECTED_COUNT, BLOCK), lambda i: (0, i)),
        scratch_shapes=[
            pltpu.VMEM(((row_span + 2) * lanes, width), jnp.bfloat16),
            pltpu.VMEM((LAYERS, 3 * width, width), jnp.bfloat16),
            pltpu.VMEM((LAYERS, width, width), jnp.bfloat16),
            pltpu.VMEM((LAYERS, ff, width), jnp.bfloat16),
            pltpu.VMEM((LAYERS, width, ff), jnp.bfloat16),
            pltpu.VMEM((3 * width, BLOCK), jnp.bfloat16),
            pltpu.VMEM((width, BLOCK), jnp.bfloat16),
        ],
        compiler_params=pltpu.CompilerParams(dimension_semantics=("arbitrary",)),
        name="members_attend",
    )(
        place,
        patches,
        bias,
        opening,
        opening_bias[None],
        following_filter,
        gains,
        query_key_value_weight,
        attention_output_weight,
        upward_weight,
        downward_weight,
        readout,
    )
    correction = correction.reshape(CORRECTED_COUNT, row_span, cols, members).transpose(3, 0, 1, 2)
    correction = lax.all_to_all(correction, "mem", split_axis=0, concat_axis=3, tiled=True)
    return member_predictors[:, :CORRECTED_COUNT].astype(jnp.float32) + correction


def solution(mesh):
    in_specs = (P("mem", None, "sp", None), P("mem", "sp", None)) + (P(),) * 10
    out_specs = P("mem", None, "sp", None)
    return jax.shard_map(shards, mesh=mesh, in_specs=in_specs, out_specs=out_specs, check_vma=False)
```

profile of v0, /device:TPU:16, one launch (start us, length us, event | category | flops | bytes accessed | tf_op | source)
XLA Modules:
  0.0 96.3 jit_solution(15495150356042292440)
XLA Ops:
  0.0 1.9 %collective-permute-start = (bf16[8,8,2,128]{3,2,1,0:T(2,128)(2,1)}, bf16[8,8,2,128]{3,2,1,0:T(2,128)(2,1)S(1)}, u32[]{:S(2)}, u32[]{:S(2)}) collective-permute-start(bf16[8,8,2,128]{3,2,1,0:T(2,128)(2,1)} %param.12), channel_id=1, source_target_pairs={{0,1},{1,2},{2,3},{3,4},{4,5},{5,6},{6,7},{8,9},{9,10},{10,11},{11... | collective-permute-start | bytes 98312 | tf_op jit(solution)/shard_map/ppermute | solution.py:25
  1.9 3.6 %collective-permute-start.1 = (bf16[8,8,2,128]{3,2,1,0:T(2,128)(2,1)}, bf16[8,8,2,128]{3,2,1,0:T(2,128)(2,1)S(1)}, u32[]{:S(2)}, u32[]{:S(2)}) collective-permute-start(bf16[8,8,2,128]{3,2,1,0:T(2,128)(2,1)} %param.12), channel_id=1, source_target_pairs={{1,0},{2,1},{3,2},{4,3},{5,4},{6,5},{7,6},{9,8},{10,9},{11,10},{12... | collective-permute-start | bytes 98312 | tf_op jit(solution)/shard_map/ppermute | solution.py:27
  5.6 0.9 fusion
  6.5 0.7 copy-done.1
  7.3 0.6 pad_bitcast_fusion.gains
  8.3 0.7 copy-done.2
  8.9 0.6 pad.19.readout
  9.6 0.2 pad_slice_fusion.1
  9.9 0.2 reshape.48
  10.0 0.2 reshape.50
  10.2 0.2 reshape.52
  10.4 0.2 reshape.54
  10.7 0.7 pad_maximum_fusion.2
  11.4 3.7 %all-to-all-start = ((bf16[4,8,1792]{2,1,0:T(8,128)(2,1)}), bf16[4,8,1792]{2,1,0:T(8,128)(2,1)S(1)}, u32[]{:S(2)}, u32[]{:S(2)}) async-start(bf16[4,8,1792]{2,1,0:T(8,128)(2,1)} %pad_maximum_fusion.2), calls=%async_computation | async-start | bytes 229376 | tf_op jit(solution)/shard_map/all_to_all | solution.py:189
  15.1 0.6 pad_add_fusion.place
  15.6 4.4 %all-to-all-done = bf16[4,8,1792]{2,1,0:T(8,128)(2,1)S(1)} async-done(((bf16[4,8,1792]{2,1,0:T(8,128)(2,1)}), bf16[4,8,1792]{2,1,0:T(8,128)(2,1)S(1)}, u32[]{:S(2)}, u32[]{:S(2)}) %all-to-all-start) | async-done | bytes 114720 | tf_op jit(solution)/shard_map/all_to_all | solution.py:189
  20.1 0.8 reshape.57
  20.9 0.7 copy.40
  21.6 0.3 reshape.58
  21.9 0.1 pad_slice_fusion.3
  22.1 0.2 copy.42
  22.3 0.6 broadcast_in_dim.9
  23.0 0.9 reshape.60.bias
  23.9 0.8 pad_maximum_fusion.patches
  24.7 59.9 %members_attend.1 = f32[2,2048]{1,0:T(2,128)} custom-call(s32[2]{0:T(128)} %pad_add_fusion.place, bf16[6,24,1152]{2,1,0:T(8,128)(2,1)} %pad_maximum_fusion.patches, bf16[16,32,128]{2,1,0:T(8,128)(2,1)} %reshape.60.bias, bf16[3,24,128]{2,1,0:T(8,128)(2,1)} %bitcast.37, f32[1,128]{1,0:T(1,128)} %bitcast.39, bf16[9,128,128]{2,1,0:T(8,128)(2,1)} %following.1, ...), custom_call_target="tpu_custom_call" | custom-call | tf_op jit(solution)/shard_map/members_attend/pallas_call | solution.py:217
  84.6 0.8 reshape.63
  85.5 0.7 reshape.64
  86.2 3.3 %all-to-all-start.1 = ((f32[4,1,1024]{2,1,0:T(1,128)}), f32[4,1,1024]{2,1,0:T(1,128)S(1)}, u32[]{:S(2)}, u32[]{:S(2)}) async-start(f32[4,1,1024]{2,1,0:T(1,128)} %reshape.64), calls=%async_computation.1 | async-start | bytes 32768 | tf_op jit(solution)/shard_map/all_to_all | solution.py:254
  89.5 4.7 %all-to-all-done.1 = f32[4,1,1024]{2,1,0:T(1,128)S(1)} async-done(((f32[4,1,1024]{2,1,0:T(1,128)}), f32[4,1,1024]{2,1,0:T(1,128)S(1)}, u32[]{:S(2)}, u32[]{:S(2)}) %all-to-all-start.1) | async-done | bytes 16416 | tf_op jit(solution)/shard_map/all_to_all | solution.py:254
  94.2 0.5 broadcast.8
  94.7 0.7 reduce
  95.7 0.6 copy.47
  (26 shorter events, 1.3 us)
Async XLA Ops:
  0.0 9.5 %collective-permute-start = (bf16[8,8,2,128]{3,2,1,0:T(2,128)(2,1)}, bf16[8,8,2,128]{3,2,1,0:T(2,128)(2,1)S(1)}, u32[]{:S(2)}, u32[]{:S(2)}) collective-permute-start(bf16[8,8,2,128]{3,2,1,0:T(2,128)(2,1)} %param.12), channel_id=1, source_target_pairs={{0,1},{1,2},{2,3},{3,4},{4,5},{5,6},{6,7},{8,9},{9,10},{10,11},{11... | collective-permute-start | bytes 98312 | tf_op jit(solution)/shard_map/ppermute | solution.py:25
  1.9 7.6 %collective-permute-start.1 = (bf16[8,8,2,128]{3,2,1,0:T(2,128)(2,1)}, bf16[8,8,2,128]{3,2,1,0:T(2,128)(2,1)S(1)}, u32[]{:S(2)}, u32[]{:S(2)}) collective-permute-start(bf16[8,8,2,128]{3,2,1,0:T(2,128)(2,1)} %param.12), channel_id=1, source_target_pairs={{1,0},{2,1},{3,2},{4,3},{5,4},{6,5},{7,6},{9,8},{10,9},{11,10},{12... | collective-permute-start | bytes 98312 | tf_op jit(solution)/shard_map/ppermute | solution.py:27
  6.5 0.7 copy-start.1
  6.5 0.7 copy-start.3
  7.9 1.6 %copy-start = (bf16[8,8,2,128]{3,2,1,0:T(2,128)(2,1)S(1)}, bf16[8,8,2,128]{3,2,1,0:T(2,128)(2,1)}, u32[]{:S(2)}) copy-start(bf16[8,8,2,128]{3,2,1,0:T(2,128)(2,1)} %param.12) | copy-start | bytes 98308
  8.3 0.7 copy-start.2
  11.4 8.7 %all-to-all-start = ((bf16[4,8,1792]{2,1,0:T(8,128)(2,1)}), bf16[4,8,1792]{2,1,0:T(8,128)(2,1)S(1)}, u32[]{:S(2)}, u32[]{:S(2)}) async-start(bf16[4,8,1792]{2,1,0:T(8,128)(2,1)} %pad_maximum_fusion.2), calls=%async_computation | async-start | bytes 229376 | tf_op jit(solution)/shard_map/all_to_all | solution.py:189
  86.2 7.9 %all-to-all-start.1 = ((f32[4,1,1024]{2,1,0:T(1,128)}), f32[4,1,1024]{2,1,0:T(1,128)S(1)}, u32[]{:S(2)}, u32[]{:S(2)}) async-start(f32[4,1,1024]{2,1,0:T(1,128)} %reshape.64), calls=%async_computation.1 | async-start | bytes 32768 | tf_op jit(solution)/shard_map/all_to_all | solution.py:254
where the time goes:
time: 96.8 us; the launch traced here: 96.3 us
  Pallas kernels  59.9 us (62%)
  starting transfers between devices  12.5 us (13%)
  local copies, waits for them, and re-layouts  11.6 us (12%)
  waiting for transfers between devices  9.09 us (9%)
  other arithmetic  2.94 us (3%)
    pallas_call x1, Pallas kernels, shards(): pl.pallas_call(functools.partial(kernel, sizes), grid=(tokens // BLOCK,),...  59.9 us
    all_to_all x1, waiting for transfers between devices, shards(): lax.all_to_all(correction, 'mem', split_axis=0, concat_axis=3, tiled=True)  4.66 us
    all_to_all x1, waiting for transfers between devices, shards(): lax.all_to_all(parcels, 'mem', split_axis=0, concat_axis=0, tiled=True)  4.42 us
    all_to_all x1, starting transfers between devices, shards(): lax.all_to_all(parcels, 'mem', split_axis=0, concat_axis=0, tiled=True)  3.72 us
    ppermute x1, starting transfers between devices, extended(): lax.ppermute(head, axis, [((i + 1) % count, i) for i in range(ends)])  3.64 us
    all_to_all x1, starting transfers between devices, shards(): lax.all_to_all(correction, 'mem', split_axis=0, concat_axis=3, tiled=True)  3.25 us
    unnamed x10, local copies, waits for them, and re-layouts  2.17 us
  transfers between devices with their start and end apart: 4, of which 2 were waited for; matrix products, arithmetic and copies ran while one was open for 3% of the time, Pallas kernels for 0%

commit v1 on v0

--- a/solution.py
+++ b/solution.py
@@ -95,8 +95,9 @@
                 total = jnp.zeros((chunk, width), jnp.float32) + opening_bias[...]
                 for off in range(3):
                     total = total + dot_first(patches[row + off, :, pl.ds(start, chunk)], opening[off])
-                col_id = place[1] - 1 + (start + lax.broadcasted_iota(jnp.int32, total.shape, 0)) // members
-                fits = (col_id >= 0) & (col_id < col_total) & row_fits
+                spot = start + lax.broadcasted_iota(jnp.int32, (chunk, 1), 0)
+                fits = (spot >= (1 - place[1]) * members) & (spot < (col_total + 1 - place[1]) * members)
+                fits = fits & row_fits
                 value = jnp.where(fits, jax.nn.gelu(total), 0.0)
                 first[pl.ds(pl.multiple_of(row * lanes + start, 128), chunk), :] = value.astype(jnp.bfloat16)
                 return carry
@@ -118,30 +119,36 @@
     stream = (features + summed).astype(jnp.bfloat16).astype(jnp.float32).T
 
     each = LANES // members
-    owner = lax.broadcasted_iota(jnp.int32, (members, LANES), 1) // members
-    holds = [owner == c for c in range(each)]
+    lane = lax.broadcasted_iota(jnp.int32, (members, LANES), 1)
+    holds = [(lane >= c * members) & (lane < (c + 1) * members) for c in range(each)]
     keeps = [jnp.where(hold, 1.0, 0.0).astype(jnp.bfloat16) for hold in holds]
     scale = 1.0 / math.sqrt(head)
     for layer in range(LAYERS):
         normed = norm_columns(stream, gains[:, 2 * layer : 2 * layer + 1])
         triple[...] = dot(qkv_t[layer], normed).astype(jnp.bfloat16)
-        for group in range(BLOCK // LANES):
-            at = slice(group * LANES, (group + 1) * LANES)
-            offset = bias[group].astype(jnp.float32)
-            for h in range(HEADS):
-                rows = slice(h * head, (h + 1) * head)
-                queries = triple[h * head : (h + 1) * head, at]
-                keys = triple[width + h * head : width + (h + 1) * head, at]
-                values = triple[2 * width + h * head : 2 * width + (h + 1) * head, at]
-                every = dot_first(keys, queries)
-                scores = every[:members]
-                for c in range(1, each):
-                    scores = jnp.where(holds[c], every[c * members : (c + 1) * members], scores)
-                scores = scores * scale + offset
-                raised = jnp.exp(scores - jnp.max(scores, 0, keepdims=True))
-                weights = (raised * (1.0 / jnp.sum(raised, 0, keepdims=True))).astype(jnp.bfloat16)
-                spread = jnp.concatenate([weights * keep for keep in keeps], axis=0)
-                attended[rows, at] = dot(values, spread).astype(jnp.bfloat16)
+        units = [
+            (group, slice(group * LANES, (group + 1) * LANES), h * head)
+            for group in range(BLOCK // LANES)
+            for h in range(HEADS)
+        ]
+        every = [
+            dot_first(triple[width + low : width + low + head, at], triple[low : low + head, at])
+            for _, at, low in units
+        ]
+        scores = []
+        for (group, at, low), square in zip(units, every):
+            kept = square[:members]
+            for c in range(1, each):
+                kept = jnp.where(holds[c], square[c * members : (c + 1) * members], kept)
+            scores.append(kept * scale + bias[group].astype(jnp.float32))
+        highest = [jnp.max(kept, 0, keepdims=True) for kept in scores]
+        raised = [jnp.exp(kept - top) for kept, top in zip(scores, highest)]
+        shares = [1.0 / jnp.sum(value, 0, keepdims=True) for value in raised]
+        weights = [(value * share).astype(jnp.bfloat16) for value, share in zip(raised, shares)]
+        for (group, at, low), weight in zip(units, weights):
+            spread = jnp.concatenate([weight * keep for keep in keeps], axis=0)
+            values = triple[2 * width + low : 2 * width + low + head, at]
+            attended[low : low + head, at] = dot(values, spread).astype(jnp.bfloat16)
         stream = stream + dot(out_t[layer], attended[...])
         normed = norm_columns(stream, gains[:, 2 * layer + 1 : 2 * layer + 2])
         hidden = jax.nn.gelu(dot(up_t[layer], normed)).astype(jnp.bfloat16)

time: 96.8 us -> 72.1 us (0.74)
  Pallas kernels: 59.9 us -> 35.3 us
    pallas_call x1, Pallas kernels: 59.9 us -> 35.3 us  [shards(): pl.pallas_call(functools.partial(kernel, sizes), grid=(tokens // BLOCK,),...]
  transfers between devices with their start and end apart: 4 -> 4, of which waited for: 2 -> 2; matrix products, arithmetic and copies ran while one was open for 3% -> 4% of each run, Pallas kernels for 0% -> 0%
where the time goes in v1:
time: 72.1 us; the launch traced here: 71.6 us
  Pallas kernels  35.3 us (49%)
  starting transfers between devices  12.5 us (17%)
  local copies, waits for them, and re-layouts  11.6 us (16%)
  waiting for transfers between devices  9.09 us (13%)
  other arithmetic  2.94 us (4%)
    pallas_call x1, Pallas kernels, shards(): pl.pallas_call(functools.partial(kernel, sizes), grid=(tokens // BLOCK,),...  35.3 us
    all_to_all x1, waiting for transfers between devices, shards(): lax.all_to_all(correction, 'mem', split_axis=0, concat_axis=3, tiled=True)  4.66 us
    all_to_all x1, waiting for transfers between devices, shards(): lax.all_to_all(parcels, 'mem', split_axis=0, concat_axis=0, tiled=True)  4.42 us
    all_to_all x1, starting transfers between devices, shards(): lax.all_to_all(parcels, 'mem', split_axis=0, concat_axis=0, tiled=True)  3.72 us
    ppermute x1, starting transfers between devices, extended(): lax.ppermute(head, axis, [((i + 1) % count, i) for i in range(ends)])  3.64 us
    all_to_all x1, starting transfers between devices, shards(): lax.all_to_all(correction, 'mem', split_axis=0, concat_axis=3, tiled=True)  3.25 us
    unnamed x10, local copies, waits for them, and re-layouts  2.17 us
    ppermute x1, starting transfers between devices, extended(): lax.ppermute(tail, axis, [(i, (i + 1) % count) for i in range(ends)])  1.91 us
  transfers between devices with their start and end apart: 4, of which 2 were waited for; matrix products, arithmetic and copies ran while one was open for 4% of the time, Pallas kernels for 0%

profile of v1, /device:TPU:16, one launch (start us, length us, event | category | flops | bytes accessed | tf_op | source)
XLA Modules:
  0.0 71.6 jit_solution(16006282945849803681)
XLA Ops:
  0.0 1.9 %collective-permute-start = (bf16[8,8,2,128]{3,2,1,0:T(2,128)(2,1)}, bf16[8,8,2,128]{3,2,1,0:T(2,128)(2,1)S(1)}, u32[]{:S(2)}, u32[]{:S(2)}) collective-permute-start(bf16[8,8,2,128]{3,2,1,0:T(2,128)(2,1)} %param.12), channel_id=1, source_target_pairs={{0,1},{1,2},{2,3},{3,4},{4,5},{5,6},{6,7},{8,9},{9,10},{10,11},{11... | collective-permute-start | bytes 98312 | tf_op jit(solution)/shard_map/ppermute | solution.py:25
  1.9 3.6 %collective-permute-start.1 = (bf16[8,8,2,128]{3,2,1,0:T(2,128)(2,1)}, bf16[8,8,2,128]{3,2,1,0:T(2,128)(2,1)S(1)}, u32[]{:S(2)}, u32[]{:S(2)}) collective-permute-start(bf16[8,8,2,128]{3,2,1,0:T(2,128)(2,1)} %param.12), channel_id=1, source_target_pairs={{1,0},{2,1},{3,2},{4,3},{5,4},{6,5},{7,6},{9,8},{10,9},{11,10},{12... | collective-permute-start | bytes 98312 | tf_op jit(solution)/shard_map/ppermute | solution.py:27
  5.6 0.9 %fusion = (bf16[8,2,32]{2,1,0:T(2,128)(2,1)S(1)}, bf16[8,2,32]{2,1,0:T(2,128)(2,1)S(1)}, bf16[8,2,32]{2,1,0:T(2,128)(2,1)S(1)}, bf16[8,2,32]{2,1,0:T(2,128)(2,1)S(1)}) fusion(bf16[8,2,128]{2,1,0:T(2,128)(2,1)} %param.13), kind=kLoop, calls=%fused_computation.16 | loop fusion | bytes 8192 | tf_op jit(solution)/shard_map/slice | solution.py:189
  6.5 0.7 copy-done.1
  7.3 0.6 pad_bitcast_fusion.gains
  8.3 0.7 copy-done.2
  8.9 0.6 pad.19.readout
  9.6 0.2 pad_slice_fusion.1
  9.9 0.2 reshape.48
  10.0 0.2 reshape.50
  10.2 0.2 reshape.52
  10.4 0.2 reshape.54
  10.7 0.7 pad_maximum_fusion.2
  11.4 3.7 %all-to-all-start = ((bf16[4,8,1792]{2,1,0:T(8,128)(2,1)}), bf16[4,8,1792]{2,1,0:T(8,128)(2,1)S(1)}, u32[]{:S(2)}, u32[]{:S(2)}) async-start(bf16[4,8,1792]{2,1,0:T(8,128)(2,1)} %pad_maximum_fusion.2), calls=%async_computation | async-start | bytes 229376 | tf_op jit(solution)/shard_map/all_to_all | solution.py:196
  15.1 0.6 pad_add_fusion.place
  15.6 4.4 %all-to-all-done = bf16[4,8,1792]{2,1,0:T(8,128)(2,1)S(1)} async-done(((bf16[4,8,1792]{2,1,0:T(8,128)(2,1)}), bf16[4,8,1792]{2,1,0:T(8,128)(2,1)S(1)}, u32[]{:S(2)}, u32[]{:S(2)}) %all-to-all-start) | async-done | bytes 114720 | tf_op jit(solution)/shard_map/all_to_all | solution.py:196
  20.1 0.8 %reshape.57 = bf16[32,8,6,36]{3,2,1,0:T(8,128)(2,1)S(1)} reshape(bf16[32,1728]{1,0:T(8,128)(2,1)S(1)} %bitcast.33) | data formatting | bytes 221184 | tf_op jit(solution)/shard_map/reshape | solution.py:200
  20.9 0.7 copy.40
  21.6 0.3 reshape.58
  21.9 0.1 pad_slice_fusion.3
  22.1 0.2 copy.42
  22.3 0.6 broadcast_in_dim.9
  23.0 0.9 %reshape.60.bias = bf16[16,32,128]{2,1,0:T(8,128)(2,1)} reshape(bf16[16,32,4,32]{3,2,1,0:T(4,128)(2,1)S(1)} %broadcast_in_dim.9) | data formatting | bytes 262144 | tf_op jit(solution)/shard_map/reshape | solution.py:213
  23.9 0.8 %pad_maximum_fusion.patches = bf16[6,24,1152]{2,1,0:T(8,128)(2,1)} fusion(bf16[6,8,1152]{2,1,0:T(8,128)(2,1)S(1)} %get-tuple-element.10, bf16[6,8,1152]{2,1,0:T(8,128)(2,1)S(1)} %get-tuple-element.9, bf16[6,8,1152]{2,1,0:T(8,128)(2,1)S(1)} %reshape.58), kind=kLoop, calls=%fused_computation | loop fusion | flops 995328 | bytes 663552 | tf_op jit(solution)/shard_map/concatenate | solution.py:207
  24.7 35.3 %members_attend.1 = f32[2,2048]{1,0:T(2,128)} custom-call(s32[2]{0:T(128)} %pad_add_fusion.place, bf16[6,24,1152]{2,1,0:T(8,128)(2,1)} %pad_maximum_fusion.patches, bf16[16,32,128]{2,1,0:T(8,128)(2,1)} %reshape.60.bias, bf16[3,24,128]{2,1,0:T(8,128)(2,1)} %bitcast.37, f32[1,128]{1,0:T(1,128)} %bitcast.39, bf16[9,128,128]{2,1,0:T(8,128)(2,1)} %following.1, ...), custom_call_target="tpu_custom_call" | custom-call | tf_op jit(solution)/shard_map/members_attend/pallas_call | solution.py:224
  59.9 0.8 %reshape.63 = f32[2,2,32,32]{3,2,1,0:T(8,128)S(1)} reshape(f32[2,2048]{1,0:T(2,128)} %members_attend.1) | data formatting | bytes 32768 | tf_op jit(solution)/shard_map/reshape | solution.py:260
  60.8 0.7 %reshape.64 = f32[4,1,1024]{2,1,0:T(1,128)} reshape(f32[32,2,2,32]{3,2,1,0:T(2,128)S(1)} %bitcast.34) | data formatting | bytes 32768
  61.6 3.3 %all-to-all-start.1 = ((f32[4,1,1024]{2,1,0:T(1,128)}), f32[4,1,1024]{2,1,0:T(1,128)S(1)}, u32[]{:S(2)}, u32[]{:S(2)}) async-start(f32[4,1,1024]{2,1,0:T(1,128)} %reshape.64), calls=%async_computation.1 | async-start | bytes 32768 | tf_op jit(solution)/shard_map/all_to_all | solution.py:261
  64.8 4.7 %all-to-all-done.1 = f32[4,1,1024]{2,1,0:T(1,128)S(1)} async-done(((f32[4,1,1024]{2,1,0:T(1,128)}), f32[4,1,1024]{2,1,0:T(1,128)S(1)}, u32[]{:S(2)}, u32[]{:S(2)}) %all-to-all-start.1) | async-done | bytes 16416 | tf_op jit(solution)/shard_map/all_to_all | solution.py:261
  69.5 0.5 broadcast.8
  70.0 0.7 reduce
  71.0 0.6 copy.47
  (26 shorter events, 1.3 us)
Async XLA Ops:
  0.0 9.5 %collective-permute-start = (bf16[8,8,2,128]{3,2,1,0:T(2,128)(2,1)}, bf16[8,8,2,128]{3,2,1,0:T(2,128)(2,1)S(1)}, u32[]{:S(2)}, u32[]{:S(2)}) collective-permute-start(bf16[8,8,2,128]{3,2,1,0:T(2,128)(2,1)} %param.12), channel_id=1, source_target_pairs={{0,1},{1,2},{2,3},{3,4},{4,5},{5,6},{6,7},{8,9},{9,10},{10,11},{11... | collective-permute-start | bytes 98312 | tf_op jit(solution)/shard_map/ppermute | solution.py:25
  1.9 7.6 %collective-permute-start.1 = (bf16[8,8,2,128]{3,2,1,0:T(2,128)(2,1)}, bf16[8,8,2,128]{3,2,1,0:T(2,128)(2,1)S(1)}, u32[]{:S(2)}, u32[]{:S(2)}) collective-permute-start(bf16[8,8,2,128]{3,2,1,0:T(2,128)(2,1)} %param.12), channel_id=1, source_target_pairs={{1,0},{2,1},{3,2},{4,3},{5,4},{6,5},{7,6},{9,8},{10,9},{11,10},{12... | collective-permute-start | bytes 98312 | tf_op jit(solution)/shard_map/ppermute | solution.py:27
  6.5 0.7 copy-start.1
  6.5 0.7 copy-start.3
  7.9 1.6 %copy-start = (bf16[8,8,2,128]{3,2,1,0:T(2,128)(2,1)S(1)}, bf16[8,8,2,128]{3,2,1,0:T(2,128)(2,1)}, u32[]{:S(2)}) copy-start(bf16[8,8,2,128]{3,2,1,0:T(2,128)(2,1)} %param.12) | copy-start | bytes 98308
  8.3 0.7 copy-start.2
  11.4 8.7 %all-to-all-start = ((bf16[4,8,1792]{2,1,0:T(8,128)(2,1)}), bf16[4,8,1792]{2,1,0:T(8,128)(2,1)S(1)}, u32[]{:S(2)}, u32[]{:S(2)}) async-start(bf16[4,8,1792]{2,1,0:T(8,128)(2,1)} %pad_maximum_fusion.2), calls=%async_computation | async-start | bytes 229376 | tf_op jit(solution)/shard_map/all_to_all | solution.py:196
  61.6 7.9 %all-to-all-start.1 = ((f32[4,1,1024]{2,1,0:T(1,128)}), f32[4,1,1024]{2,1,0:T(1,128)S(1)}, u32[]{:S(2)}, u32[]{:S(2)}) async-start(f32[4,1,1024]{2,1,0:T(1,128)} %reshape.64), calls=%async_computation.1 | async-start | bytes 32768 | tf_op jit(solution)/shard_map/all_to_all | solution.py:261

commit v2 on v1

--- a/solution.py
+++ b/solution.py
@@ -12,7 +12,7 @@
 HEADS = 8
 LAYERS = 2
 LANES = 128
-BLOCK = 256
+BLOCK = 512
 
 
 def extended(cells, axis, dim, width):
@@ -113,9 +113,8 @@
         return first[pl.ds(pl.multiple_of(start, members), BLOCK), :]
 
     features = shifted(1, 1).astype(jnp.float32)
-    summed = jnp.zeros((BLOCK, width), jnp.float32)
-    for tap in range(9):
-        summed = summed + dot(shifted(tap // 3, tap % 3), following[tap])
+    taps = jnp.concatenate([shifted(tap // 3, tap % 3) for tap in range(9)], axis=1)
+    summed = dot(taps, following[...])
     stream = (features + summed).astype(jnp.bfloat16).astype(jnp.float32).T
 
     each = LANES // members
@@ -249,7 +248,7 @@
         bias,
         opening,
         opening_bias[None],
-        following_filter,
+        following_filter.reshape(9 * width, width),
         gains,
         query_key_value_weight,
         attention_output_weight,

time: 72.1 us -> 60.6 us (0.84)
  Pallas kernels: 35.3 us -> 23.8 us
    pallas_call x1, Pallas kernels: 35.3 us -> 23.8 us  [shards(): pl.pallas_call(functools.partial(kernel, sizes), grid=(tokens // BLOCK,),...]
  transfers between devices with their start and end apart: 4 -> 4, of which waited for: 2 -> 2; matrix products, arithmetic and copies ran while one was open for 4% -> 5% of each run, Pallas kernels for 0% -> 0%
where the time goes in v2:
time: 60.6 us; the launch traced here: 60.1 us
  Pallas kernels  23.8 us (39%)
  starting transfers between devices  12.5 us (21%)
  local copies, waits for them, and re-layouts  11.6 us (19%)
  waiting for transfers between devices  9.09 us (15%)
  other arithmetic  2.94 us (5%)
    pallas_call x1, Pallas kernels, shards(): pl.pallas_call(functools.partial(kernel, sizes), grid=(tokens // BLOCK,),...  23.8 us
    all_to_all x1, waiting for transfers between devices, shards(): lax.all_to_all(correction, 'mem', split_axis=0, concat_axis=3, tiled=True)  4.66 us
    all_to_all x1, waiting for transfers between devices, shards(): lax.all_to_all(parcels, 'mem', split_axis=0, concat_axis=0, tiled=True)  4.42 us
    all_to_all x1, starting transfers between devices, shards(): lax.all_to_all(parcels, 'mem', split_axis=0, concat_axis=0, tiled=True)  3.72 us
    ppermute x1, starting transfers between devices, extended(): lax.ppermute(head, axis, [((i + 1) % count, i) for i in range(ends)])  3.64 us
    all_to_all x1, starting transfers between devices, shards(): lax.all_to_all(correction, 'mem', split_axis=0, concat_axis=3, tiled=True)  3.25 us
    unnamed x10, local copies, waits for them, and re-layouts  2.17 us
    ppermute x1, starting transfers between devices, extended(): lax.ppermute(tail, axis, [(i, (i + 1) % count) for i in range(ends)])  1.91 us
  transfers between devices with their start and end apart: 4, of which 2 were waited for; matrix products, arithmetic and copies ran while one was open for 5% of the time, Pallas kernels for 0%

profile of v2, /device:TPU:16, one launch (start us, length us, event | category | flops | bytes accessed | tf_op | source)
XLA Modules:
  0.0 60.1 jit_solution(810999496916362749)
XLA Ops:
  0.0 1.9 %collective-permute-start = (bf16[8,8,2,128]{3,2,1,0:T(2,128)(2,1)}, bf16[8,8,2,128]{3,2,1,0:T(2,128)(2,1)S(1)}, u32[]{:S(2)}, u32[]{:S(2)}) collective-permute-start(bf16[8,8,2,128]{3,2,1,0:T(2,128)(2,1)} %param.12), channel_id=1, source_target_pairs={{0,1},{1,2},{2,3},{3,4},{4,5},{5,6},{6,7},{8,9},{9,10},{10,11},{11... | collective-permute-start | bytes 98312 | tf_op jit(solution)/shard_map/ppermute | solution.py:25
  1.9 3.6 %collective-permute-start.1 = (bf16[8,8,2,128]{3,2,1,0:T(2,128)(2,1)}, bf16[8,8,2,128]{3,2,1,0:T(2,128)(2,1)S(1)}, u32[]{:S(2)}, u32[]{:S(2)}) collective-permute-start(bf16[8,8,2,128]{3,2,1,0:T(2,128)(2,1)} %param.12), channel_id=1, source_target_pairs={{1,0},{2,1},{3,2},{4,3},{5,4},{6,5},{7,6},{9,8},{10,9},{11,10},{12... | collective-permute-start | bytes 98312 | tf_op jit(solution)/shard_map/ppermute | solution.py:27
  5.6 0.9 %fusion = (bf16[8,2,32]{2,1,0:T(2,128)(2,1)S(1)}, bf16[8,2,32]{2,1,0:T(2,128)(2,1)S(1)}, bf16[8,2,32]{2,1,0:T(2,128)(2,1)S(1)}, bf16[8,2,32]{2,1,0:T(2,128)(2,1)S(1)}) fusion(bf16[8,2,128]{2,1,0:T(2,128)(2,1)} %param.13), kind=kLoop, calls=%fused_computation.16 | loop fusion | bytes 8192 | tf_op jit(solution)/shard_map/slice | solution.py:188
  6.5 0.7 %copy-done.1 = f32[2,2,128]{2,1,0:T(2,128)S(1)} copy-done((f32[2,2,128]{2,1,0:T(2,128)S(1)}, f32[2,2,128]{2,1,0:T(2,128)}, u32[]{:S(2)}) %copy-start.1) | copy-done | bytes 2072
  7.3 0.6 %pad_bitcast_fusion.gains = f32[128,8]{1,0:T(8,128)} fusion(f32[5,128]{0,1:T(8,128)S(1)} %copy.43), kind=kLoop, calls=%fused_computation.8 | loop fusion | bytes 6656 | tf_op jit(solution)/shard_map/transpose | solution.py:216
  8.3 0.7 %copy-done.2 = bf16[128,2]{0,1:T(2,128)(2,1)S(1)} copy-done((bf16[128,2]{0,1:T(2,128)(2,1)S(1)}, bf16[128,2]{0,1:T(2,128)(2,1)}, u32[]{:S(2)}) %copy-start.2) | copy-done | bytes 536
  8.9 0.6 pad.19.readout
  9.6 0.2 pad_slice_fusion.1
  9.9 0.2 reshape.51
  10.0 0.2 reshape.53
  10.2 0.2 reshape.55
  10.4 0.2 reshape.57
  10.7 0.7 %pad_maximum_fusion.2 = bf16[4,8,1792]{2,1,0:T(8,128)(2,1)} fusion(bf16[1,8,1792]{2,1,0:T(8,128)(2,1)S(1)} %get-tuple-element.18, bf16[1,8,1792]{2,1,0:T(8,128)(2,1)S(1)} %get-tuple-element.17, bf16[1,8,1792]{2,1,0:T(8,128)(2,1)S(1)} %get-tuple-element.16, bf16[1,8,1792]{2,1,0:T(8,128)(2,1)S(1)} %get-tuple-element.15), kind=kLoop, calls=%fused_computation.4 | loop fusion | flops 172032 | bytes 229376 | tf_op jit(solution)/shard_map/stack | solution.py:183
  11.4 3.7 %all-to-all-start = ((bf16[4,8,1792]{2,1,0:T(8,128)(2,1)}), bf16[4,8,1792]{2,1,0:T(8,128)(2,1)S(1)}, u32[]{:S(2)}, u32[]{:S(2)}) async-start(bf16[4,8,1792]{2,1,0:T(8,128)(2,1)} %pad_maximum_fusion.2), calls=%async_computation | async-start | bytes 229376 | tf_op jit(solution)/shard_map/all_to_all | solution.py:195
  15.1 0.6 pad_add_fusion.place
  15.6 4.4 %all-to-all-done = bf16[4,8,1792]{2,1,0:T(8,128)(2,1)S(1)} async-done(((bf16[4,8,1792]{2,1,0:T(8,128)(2,1)}), bf16[4,8,1792]{2,1,0:T(8,128)(2,1)S(1)}, u32[]{:S(2)}, u32[]{:S(2)}) %all-to-all-start) | async-done | bytes 114720 | tf_op jit(solution)/shard_map/all_to_all | solution.py:195
  20.1 0.8 %reshape.60 = bf16[32,8,6,36]{3,2,1,0:T(8,128)(2,1)S(1)} reshape(bf16[32,1728]{1,0:T(8,128)(2,1)S(1)} %bitcast.34) | data formatting | bytes 221184 | tf_op jit(solution)/shard_map/reshape | solution.py:199
  20.9 0.7 %copy.40 = bf16[6,8,36,32]{3,2,1,0:T(8,128)(2,1)S(1)} copy(bf16[6,8,36,32]{2,0,1,3:T(8,128)(2,1)S(1)} %bitcast.32) | data formatting | bytes 221184 | tf_op jit(solution)/shard_map/transpose | solution.py:204
  21.6 0.3 reshape.61
  21.9 0.1 pad_slice_fusion.3
  22.1 0.2 copy.42
  22.3 0.6 %broadcast_in_dim.9 = bf16[16,32,4,32]{3,2,1,0:T(4,128)(2,1)S(1)} broadcast(bf16[16,32,4]{2,1,0:T(8,128)(2,1)S(1)} %copy.42), dimensions={0,1,2} | broadcast | bytes 135168 | tf_op jit(solution)/shard_map/broadcast_in_dim | solution.py:212
  23.0 0.9 %reshape.63.bias = bf16[16,32,128]{2,1,0:T(8,128)(2,1)} reshape(bf16[16,32,4,32]{3,2,1,0:T(4,128)(2,1)S(1)} %broadcast_in_dim.9) | data formatting | bytes 262144 | tf_op jit(solution)/shard_map/reshape | solution.py:212
  23.9 0.8 %pad_maximum_fusion.patches = bf16[6,24,1152]{2,1,0:T(8,128)(2,1)} fusion(bf16[6,8,1152]{2,1,0:T(8,128)(2,1)S(1)} %get-tuple-element.10, bf16[6,8,1152]{2,1,0:T(8,128)(2,1)S(1)} %get-tuple-element.9, bf16[6,8,1152]{2,1,0:T(8,128)(2,1)S(1)} %reshape.61), kind=kLoop, calls=%fused_computation | loop fusion | flops 995328 | bytes 663552 | tf_op jit(solution)/shard_map/concatenate | solution.py:206
  24.7 23.8 %members_attend.1 = f32[2,2048]{1,0:T(2,128)} custom-call(s32[2]{0:T(128)} %pad_add_fusion.place, bf16[6,24,1152]{2,1,0:T(8,128)(2,1)} %pad_maximum_fusion.patches, bf16[16,32,128]{2,1,0:T(8,128)(2,1)} %reshape.63.bias, bf16[3,24,128]{2,1,0:T(8,128)(2,1)} %bitcast.39, f32[1,128]{1,0:T(1,128)} %bitcast.41, bf16[1152,128]{1,0:T(8,128)(2,1)} %bitcast.35, ...), custom_call_target="tpu_custom_call" | custom-call | tf_op jit(solution)/shard_map/members_attend/pallas_call | solution.py:223
  48.5 0.8 %reshape.67 = f32[2,2,32,32]{3,2,1,0:T(8,128)S(1)} reshape(f32[2,2048]{1,0:T(2,128)} %members_attend.1) | data formatting | bytes 32768 | tf_op jit(solution)/shard_map/reshape | solution.py:259
  49.4 0.7 %reshape.68 = f32[4,1,1024]{2,1,0:T(1,128)} reshape(f32[32,2,2,32]{3,2,1,0:T(2,128)S(1)} %bitcast.36) | data formatting | bytes 32768
  50.1 3.3 %all-to-all-start.1 = ((f32[4,1,1024]{2,1,0:T(1,128)}), f32[4,1,1024]{2,1,0:T(1,128)S(1)}, u32[]{:S(2)}, u32[]{:S(2)}) async-start(f32[4,1,1024]{2,1,0:T(1,128)} %reshape.68), calls=%async_computation.1 | async-start | bytes 32768 | tf_op jit(solution)/shard_map/all_to_all | solution.py:260
  53.4 4.7 %all-to-all-done.1 = f32[4,1,1024]{2,1,0:T(1,128)S(1)} async-done(((f32[4,1,1024]{2,1,0:T(1,128)}), f32[4,1,1024]{2,1,0:T(1,128)S(1)}, u32[]{:S(2)}, u32[]{:S(2)}) %all-to-all-start.1) | async-done | bytes 16416 | tf_op jit(solution)/shard_map/all_to_all | solution.py:260
  58.0 0.5 broadcast.8
  58.6 0.7 %reduce = f32[4,1024]{1,0:T(4,128)S(1)} reduce(f32[4,1,1024]{2,1,0:T(1,128)S(1)} %all-to-all-done.1, f32[]{:T(128)} %broadcast.8), dimensions={1}, to_apply=%all_to_all.17.reduce_sub_computation | reduce | bytes 32772 | tf_op jit(solution)/shard_map/all_to_all | solution.py:260
  59.5 0.6 %copy.47 = f32[8,2,2,128]{3,2,1,0:T(2,128)} copy(f32[8,2,2,128]{3,0,2,1:T(8,128)S(1)} %convert_add_fusion) | data formatting | bytes 32768 | tf_op jit(solution)/shard_map/add | solution.py:261
  (26 shorter events, 1.3 us)
Async XLA Ops:
  0.0 9.5 %collective-permute-start = (bf16[8,8,2,128]{3,2,1,0:T(2,128)(2,1)}, bf16[8,8,2,128]{3,2,1,0:T(2,128)(2,1)S(1)}, u32[]{:S(2)}, u32[]{:S(2)}) collective-permute-start(bf16[8,8,2,128]{3,2,1,0:T(2,128)(2,1)} %param.12), channel_id=1, source_target_pairs={{0,1},{1,2},{2,3},{3,4},{4,5},{5,6},{6,7},{8,9},{9,10},{10,11},{11... | collective-permute-start | bytes 98312 | tf_op jit(solution)/shard_map/ppermute | solution.py:25
  1.9 7.6 %collective-permute-start.1 = (bf16[8,8,2,128]{3,2,1,0:T(2,128)(2,1)}, bf16[8,8,2,128]{3,2,1,0:T(2,128)(2,1)S(1)}, u32[]{:S(2)}, u32[]{:S(2)}) collective-permute-start(bf16[8,8,2,128]{3,2,1,0:T(2,128)(2,1)} %param.12), channel_id=1, source_target_pairs={{1,0},{2,1},{3,2},{4,3},{5,4},{6,5},{7,6},{9,8},{10,9},{11,10},{12... | collective-permute-start | bytes 98312 | tf_op jit(solution)/shard_map/ppermute | solution.py:27
  6.5 0.7 %copy-start.1 = (f32[2,2,128]{2,1,0:T(2,128)S(1)}, f32[2,2,128]{2,1,0:T(2,128)}, u32[]{:S(2)}) copy-start(f32[2,2,128]{2,1,0:T(2,128)} %param.17) | copy-start | bytes 6148
  6.5 0.7 %copy-start.3 = (f32[128]{0:T(128)S(1)}, f32[128]{0:T(128)}, u32[]{:S(2)}) copy-start(f32[128]{0:T(128)} %param.22) | copy-start | bytes 1540
  7.9 1.6 %copy-start = (bf16[8,8,2,128]{3,2,1,0:T(2,128)(2,1)S(1)}, bf16[8,8,2,128]{3,2,1,0:T(2,128)(2,1)}, u32[]{:S(2)}) copy-start(bf16[8,8,2,128]{3,2,1,0:T(2,128)(2,1)} %param.12) | copy-start | bytes 98308
  8.3 0.7 %copy-start.2 = (bf16[128,2]{0,1:T(2,128)(2,1)S(1)}, bf16[128,2]{0,1:T(2,128)(2,1)}, u32[]{:S(2)}) copy-start(bf16[128,2]{0,1:T(2,128)(2,1)} %param.23) | copy-start | bytes 1540
  11.4 8.7 %all-to-all-start = ((bf16[4,8,1792]{2,1,0:T(8,128)(2,1)}), bf16[4,8,1792]{2,1,0:T(8,128)(2,1)S(1)}, u32[]{:S(2)}, u32[]{:S(2)}) async-start(bf16[4,8,1792]{2,1,0:T(8,128)(2,1)} %pad_maximum_fusion.2), calls=%async_computation | async-start | bytes 229376 | tf_op jit(solution)/shard_map/all_to_all | solution.py:195
  50.1 7.9 %all-to-all-start.1 = ((f32[4,1,1024]{2,1,0:T(1,128)}), f32[4,1,1024]{2,1,0:T(1,128)S(1)}, u32[]{:S(2)}, u32[]{:S(2)}) async-start(f32[4,1,1024]{2,1,0:T(1,128)} %reshape.68), calls=%async_computation.1 | async-start | bytes 32768 | tf_op jit(solution)/shard_map/all_to_all | solution.py:260
